TPU v7x, 256 devices: a whole 4x4x8 slice. The times are simulated.
256 devices in a mesh: pair: 64 (over y, z, core), aux: 4 (over x).
Axes of the slice: x: 4, y: 4, z: 8, core: 2. Of those that a mesh axis runs over, the one named last changes fastest.
Arguments:
- factors: bfloat16 [64, 8192, 8, 128], P('pair', 'aux'), may hold values from -0.0625 to 0.0625
- amplitudes: bfloat16 [3072, 128, 128], P('pair'), may hold values from -6 to 6
- block_list: int32 [3072, 3], P('pair'), may hold values from 0 to 63, as said below
- owner_map: int32 [64], replicated, may hold values from 0 to 63, as said below
Outputs:
- residual_blocks: bfloat16 [3072, 128, 128], P('pair')
Inputs may be any that keep to these rules, and one draw needn't show every extreme that they name: `block_list`: each row (k, A, C) names an occupied orbital below 64 and two virtual blocks below 8; no row repeats. Among the 48 rows of one device at most 2 have orbitals with the same owner_map entry, and exactly 2 for some entry on every device. `owner_map`: A permutation: entry k is the row of factors that holds orbital k.
All inputs are finite; a program needn't handle non-finite values.
Results may differ from a plain program's by a relative error of at most 0.0046.
Values may be sent and summed in bfloat16 or wider, within the bound.
A program may use at most 64 MiB of HBM per device.

v0:
```python
import jax
import jax.numpy as jnp
from jax import lax
from jax.sharding import PartitionSpec as P

CAP = 2


def on_device(factors, amplitudes, block_list, owner_map):
    pair_count = lax.axis_size("pair")
    slot_total = pair_count * CAP
    block_count = amplitudes.shape[0]
    block_width = amplitudes.shape[1]
    virt_blocks = factors.shape[2]
    share_rows = factors.shape[1]
    orbital_total = owner_map.shape[0]
    orbitals = block_list[:, 0]
    block_a = block_list[:, 1]
    block_c = block_list[:, 2]
    matches = orbitals[:, None] == lax.iota(jnp.int32, orbital_total)[None, :]
    owners = jnp.sum(jnp.where(matches, owner_map[None, :], 0), axis=1)
    owner_hits = (owners[:, None] == lax.iota(jnp.int32, pair_count)[None, :]).astype(jnp.int32)
    earlier = jnp.cumsum(owner_hits, axis=0) - owner_hits
    slot_rank = jnp.sum(earlier * owner_hits, axis=1)
    slots = owners * CAP + slot_rank
    placing = slots[:, None] == lax.iota(jnp.int32, slot_total)[None, :]
    place_matrix = placing.astype(jnp.bfloat16)
    flat_blocks = amplitudes.reshape(block_count, block_width * block_width)
    send_blocks = jnp.einsum(
        "js,jm->sm", place_matrix, flat_blocks, preferred_element_type=jnp.float32
    )
    send_blocks = send_blocks.astype(jnp.bfloat16).reshape(
        pair_count, CAP, block_width, block_width
    )
    send_a = jnp.sum(jnp.where(placing, block_a[:, None] + 1, 0), axis=0)
    send_c = jnp.sum(jnp.where(placing, block_c[:, None] + 1, 0), axis=0)
    send_index = (
        jnp.stack([send_a, send_c], axis=-1).astype(jnp.bfloat16).reshape(pair_count, CAP, 2)
    )
    recv_blocks, recv_index = (
        lax.all_to_all(send_blocks, "pair", split_axis=0, concat_axis=0, tiled=True),
        lax.all_to_all(send_index, "pair", split_axis=0, concat_axis=0, tiled=True),
    )
    recv_index = recv_index.reshape(slot_total, 2).astype(jnp.int32) - 1
    slot_a = recv_index[:, 0]
    slot_c = recv_index[:, 1]
    onehot_a = (slot_a[:, None] == lax.iota(jnp.int32, virt_blocks)[None, :]).astype(jnp.bfloat16)
    onehot_c = (slot_c[:, None] == lax.iota(jnp.int32, virt_blocks)[None, :]).astype(jnp.bfloat16)
    combined = (onehot_c[:, :, None] * onehot_a[:, None, :]).reshape(
        slot_total, virt_blocks * virt_blocks
    )
    recv_flat = recv_blocks.reshape(slot_total, block_width * block_width)
    weights = jnp.einsum("sm,sn->mn", combined, recv_flat, preferred_element_type=jnp.float32)
    weights = weights.reshape(virt_blocks, virt_blocks, block_width, block_width)
    weights = jnp.transpose(weights, (0, 3, 1, 2)).reshape(
        virt_blocks * block_width, virt_blocks * block_width
    )
    weights = weights.astype(jnp.bfloat16)
    factor_flat = factors.reshape(share_rows, virt_blocks * block_width)
    factor_rows = factor_flat
    inter_share = lax.psum_scatter(
        jnp.dot(factor_rows, weights, preferred_element_type=jnp.float32),
        "pair",
        scatter_dimension=0,
        tiled=True,
    )
    inter_share = inter_share.astype(jnp.bfloat16)
    shard_rows = lax.all_gather(inter_share, "pair", axis=0, tiled=True)
    height = shard_rows.shape[0]
    factor_rows = factor_flat
    left = shard_rows.reshape(height, virt_blocks, block_width)
    right = factor_rows.reshape(height, virt_blocks, block_width)
    projected = jnp.einsum("qAa,qCc->ACac", left, right, preferred_element_type=jnp.float32)
    safe_a = jnp.maximum(slot_a, 0)
    safe_c = jnp.maximum(slot_c, 0)
    summed = lax.psum(projected, "aux")
    picked = summed[safe_a, safe_c].astype(jnp.bfloat16)
    picked = picked.reshape(pair_count, CAP, block_width, block_width)
    returned = lax.all_to_all(picked, "pair", split_axis=0, concat_axis=0, tiled=True)
    returned = returned.reshape(slot_total, block_width * block_width)
    result = jnp.einsum("js,sm->jm", place_matrix, returned, preferred_element_type=jnp.float32)
    return result.astype(jnp.bfloat16).reshape(block_count, block_width, block_width)


def solution(mesh):
    placed = (P("pair", "aux", None, None), P("pair", None, None), P("pair", None), P())
    return jax.shard_map(
        on_device, mesh=mesh, in_specs=placed, out_specs=P("pair", None, None), check_vma=False
    )
```

profile of v0, /device:TPU:1, one launch (start us, length us, event | category | flops | bytes accessed | tf_op | source)
XLA Modules:
  0.0 617.8 jit_solution(2545537378293932037)
XLA Ops:
  6.5 0.8 add_bitcast_fusion
  7.3 0.8 select_reduce_fusion.3
  8.2 0.1 fusion.18
  8.2 0.1 reduce_window_sum.11
  8.3 0.2 select_reduce_fusion.2
  8.5 0.1 select_reduce_fusion.1
  8.7 0.1 stack.10
  8.8 0.2 stack.9
  9.0 0.7 copy.26
  9.6 13.2 %all-to-all-start = ((bf16[64,2,2]{1,2,0:T(2,128)(2,1)}), bf16[64,2,2]{1,2,0:T(2,128)(2,1)S(1)}, u32[]{:S(2)}, u32[]{:S(2)}) async-start(bf16[64,2,2]{1,2,0:T(2,128)(2,1)} %copy.26), calls=%async_computation | async-start | bytes 65536 | tf_op jit(solution)/shard_map/all_to_all | solution.py:42
  22.8 2.8 fusion.10
  25.6 3.2 copy.39
  28.8 3.2 all-to-all-done
  32.0 7.3 %all-to-all-start.1 = ((bf16[64,2,128,128]{3,2,1,0:T(8,128)(2,1)}), bf16[64,2,128,128]{3,2,1,0:T(8,128)(2,1)}, u32[]{:S(2)}, u32[]{:S(2)}) async-start(bf16[64,2,128,128]{3,2,1,0:T(8,128)(2,1)} %bitcast.84), calls=%async_computation.1 | async-start | bytes 8388608 | tf_op jit(solution)/shard_map/all_to_all | solution.py:41
  39.3 0.2 reduce-scatter.4.cloned.1.call-start
  39.6 0.1 copy.27
  39.7 0.1 copy.28
  39.8 0.1 sub.11
  40.0 95.3 %all-to-all-done.1 = bf16[64,2,128,128]{3,2,1,0:T(8,128)(2,1)} async-done(((bf16[64,2,128,128]{3,2,1,0:T(8,128)(2,1)}), bf16[64,2,128,128]{3,2,1,0:T(8,128)(2,1)}, u32[]{:S(2)}, u32[]{:S(2)}) %all-to-all-start.1) | async-done | bytes 4194336 | tf_op jit(solution)/shard_map/all_to_all | solution.py:41
  135.2 7.7 %copy.70 = bf16[16,8,128,128]{3,1,2,0:T(8,128)(2,1)} copy(bf16[16,8,128,128]{3,2,1,0:T(8,128)(2,1)} %bitcast.39) | data formatting | bytes 8388608
  142.9 6.4 %copy.29 = bf16[128,16384]{0,1:T(8,128)(2,1)} copy(bf16[128,16384]{1,0:T(8,128)(2,1)} %bitcast.88) | data formatting | bytes 8388608 | tf_op jit(solution)/shard_map/reshape | solution.py:52
  149.3 3.8 convert_bitcast_fusion
  153.1 3.3 copy.30
  156.3 10.6 %convolution_bitcast_fusion = f32[2048,1024]{0,1:T(8,128)} fusion(bf16[256,8,8,128]{3,2,1,0:T(8,128)(2,1)} %bitcast.92, bf16[128,8,8,128]{3,2,1,0:T(8,128)(2,1)} %bitcast.90), kind=kOutput, calls=%fused_computation.3 | convolution fusion | flops 4294967296 | bytes 14680064 | tf_op jit(solution)/shard_map/dot_general | solution.py:62
  166.9 9.3 %copy.36 = f32[2048,1024]{1,0:T(8,128)} copy(f32[2048,1024]{0,1:T(8,128)} %convolution_bitcast_fusion) | data formatting | bytes 16777216
  176.2 0.0 reduce-scatter.4.cloned.1.call-update
  176.2 0.3 all-gather.2.cloned.1.call-start
  176.5 143.6 %reduce-scatter.4.cloned.1.call-done = f32[32,1024]{1,0:T(8,128)} async-done(((f32[2048,1024]{1,0:T(8,128)}), f32[32,1024]{1,0:T(8,128)}) %reduce-scatter.4.cloned.1.call-update) | async-done | bytes 131088 | tf_op jit(solution)/shard_map/reduce_scatter | solution.py:61
  320.2 1.5 convert_element_type.57
  321.7 0.0 all-gather.2.cloned.1.call-update
  321.7 83.6 %all-gather.2.cloned.1.call-done = bf16[2048,1024]{1,0:T(8,128)(2,1)} async-done(((bf16[32,1024]{1,0:T(8,128)(2,1)}), bf16[2048,1024]{1,0:T(8,128)(2,1)}) %all-gather.2.cloned.1.call-update) | async-done | bytes 4194320 | tf_op jit(solution)/shard_map/all_gather | solution.py:68
  405.3 6.5 %copy.32 = bf16[2048,1024]{0,1:T(8,128)(2,1)} copy(bf16[2048,1024]{1,0:T(8,128)(2,1)} %all-gather.2.cloned.1.call-done) | data formatting | bytes 8388608 | tf_op jit(solution)/shard_map/all_gather | solution.py:68
  411.8 9.9 %fusion.7 = f32[8,8,128,128]{3,2,1,0:T(8,128)} fusion(bf16[2048,8,128,1]{0,2,3,1:T(8,128)(2,1)} %bitcast.89, bf16[2048,8,128]{2,1,0:T(8,128)(2,1)} %bitcast.93), kind=kOutput, calls=%fused_computation.12 | convolution fusion | flops 4294967296 | bytes 12582912 | tf_op jit(solution)/shard_map/qAa,qCc->ACac/dot_general | solution.py:73
  421.7 78.1 %all-reduce.1 = bf16[8,8,128,128]{3,2,1,0:T(8,128)(2,1)S(1)} all-reduce(f32[8,8,128,128]{3,2,1,0:T(8,128)} %fusion.7), channel_id=1, replica_groups=mesh['pair'=64,'aux'=4] {'aux'}, use_global_device_ids=true, to_apply=%region_6.7 | all-reduce | flops 1048576 | bytes 6291456 | tf_op jit(solution)/shard_map/psum | solution.py:76
  499.8 3.1 gather_fusion
  502.8 103.9 %all_to_all.15 = bf16[64,2,128,128]{3,2,1,0:T(8,128)(2,1)S(1)} all-to-all(bf16[64,2,128,128]{3,2,1,0:T(8,128)(2,1)} %bitcast.86), channel_id=1, replica_groups=mesh['pair'=64,'aux'=4] {'pair'}, dimensions={0} | all-to-all | bytes 8388608 | tf_op jit(solution)/shard_map/all_to_all | solution.py:79
  606.7 2.7 fusion.15
  609.4 1.6 copy.44
  (7 shorter events, 0.1 us)
Async XLA Ops:
  9.6 22.4 %all-to-all-start = ((bf16[64,2,2]{1,2,0:T(2,128)(2,1)}), bf16[64,2,2]{1,2,0:T(2,128)(2,1)S(1)}, u32[]{:S(2)}, u32[]{:S(2)}) async-start(bf16[64,2,2]{1,2,0:T(2,128)(2,1)} %copy.26), calls=%async_computation | async-start | bytes 65536 | tf_op jit(solution)/shard_map/all_to_all | solution.py:42
  32.0 103.2 %all-to-all-start.1 = ((bf16[64,2,128,128]{3,2,1,0:T(8,128)(2,1)}), bf16[64,2,128,128]{3,2,1,0:T(8,128)(2,1)}, u32[]{:S(2)}, u32[]{:S(2)}) async-start(bf16[64,2,128,128]{3,2,1,0:T(8,128)(2,1)} %bitcast.84), calls=%async_computation.1 | async-start | bytes 8388608 | tf_op jit(solution)/shard_map/all_to_all | solution.py:41
  39.3 280.8 %reduce-scatter.4.cloned.1.call-start = ((), (), s32[]{:S(2)}) async-start(), calls=%async_computation.5 | async-start | bytes 8519680 | tf_op jit(solution)/shard_map/reduce_scatter | solution.py:61
  176.2 229.1 %all-gather.2.cloned.1.call-start = ((), (), s32[]{:S(2)}) async-start(), calls=%async_computation.4 | async-start | bytes 4259840 | tf_op jit(solution)/shard_map/all_gather | solution.py:68
Sparse Core Ops, SparseCore 0:
  176.4 143.7 reduce-scatter.3
  323.3 81.9 all-gather.1
where the time goes:
time: 619 us; the launch traced here: 618 us
  waiting for transfers between devices  326 us (53%)
  blocking collectives  182 us (29%)
  local copies, waits for them, and re-layouts  42.2 us (7%)
  matrix products  29.8 us (5%)
  starting transfers between devices  21 us (3%)
  between operations  13.5 us (2%)
    reduce_scatter x1, waiting for transfers between devices, on_device(): lax.psum_scatter(jnp.dot(factor_rows, weights, preferred_element_type=jnp...  144 us
    all_to_all x1, blocking collectives, on_device(): lax.all_to_all(picked, 'pair', split_axis=0, concat_axis=0, tiled=True)  104 us
    all_to_all x1, waiting for transfers between devices, on_device(): lax.all_to_all(send_blocks, 'pair', split_axis=0, concat_axis=0, tiled=True)  95.3 us
    all_gather x1, waiting for transfers between devices, on_device(): shard_rows = lax.all_gather(inter_share, 'pair', axis=0, tiled=True)  83.6 us
    psum x1, blocking collectives, on_device(): summed = lax.psum(projected, 'aux')  78.1 us
    unnamed x4, local copies, waits for them, and re-layouts  21.7 us
    all_to_all x1, starting transfers between devices, on_device(): lax.all_to_all(send_index, 'pair', split_axis=0, concat_axis=0, tiled=True)  13.2 us
  transfers between devices with their start and end apart: 4, of which 4 were waited for; matrix products, arithmetic and copies ran while one was open for 1% of the time, Pallas kernels for 0%

commit v1 on v0

--- a/solution.py
+++ b/solution.py
@@ -4,6 +4,22 @@
 from jax.sharding import PartitionSpec as P
 
 CAP = 2
+
+
+def update_positions(content):
+    axis_total = jax.lax.axis_size("aux")
+
+    def watch_the_field(shaped, before):
+        if before >= axis_total:
+            return shaped
+        kept_arr = watch_the_field(
+            shaped + jax.lax.ppermute(shaped, "aux", [(c, c ^ before) for c in range(axis_total)]),
+            2 * before,
+        )
+        return kept_arr
+
+    a_next = watch_the_field(content, 1)
+    return a_next
 
 
 def on_device(factors, amplitudes, block_list, owner_map):
@@ -73,7 +89,7 @@
     projected = jnp.einsum("qAa,qCc->ACac", left, right, preferred_element_type=jnp.float32)
     safe_a = jnp.maximum(slot_a, 0)
     safe_c = jnp.maximum(slot_c, 0)
-    summed = lax.psum(projected, "aux")
+    summed = update_positions(projected)
     picked = summed[safe_a, safe_c].astype(jnp.bfloat16)
     picked = picked.reshape(pair_count, CAP, block_width, block_width)
     returned = lax.all_to_all(picked, "pair", split_axis=0, concat_axis=0, tiled=True)

time: 619 us -> 725 us (1.17)
  waiting for transfers between devices: 326 us -> 506 us
  blocking collectives: 182 us -> 104 us
    ppermute x0 -> x2, waiting for transfers between devices: none -> 181 us  [watch_the_field(): jax.lax.ppermute(shaped, 'aux', [(c, c ^ before) for c in range(axis_tota...]
    psum x1 -> x0, blocking collectives: 78.1 us -> none  [on_device(): summed = lax.psum(projected, 'aux')]
  transfers between devices with their start and end apart: 4 -> 6, of which waited for: 4 -> 6; matrix products, arithmetic and copies ran while one was open for 1% -> 1% of each run, Pallas kernels for 0% -> 0%
where the time goes in v1:
time: 725 us; the launch traced here: 724 us
  waiting for transfers between devices  506 us (70%)
  blocking collectives  104 us (14%)
  local copies, waits for them, and re-layouts  42.3 us (6%)
  matrix products  27.4 us (4%)
  starting transfers between devices  25 us (3%)
  between operations  13.6 us (2%)
    ppermute x2, waiting for transfers between devices, watch_the_field(): jax.lax.ppermute(shaped, 'aux', [(c, c ^ before) for c in range(axis_tota...  181 us
    reduce_scatter x1, waiting for transfers between devices, on_device(): lax.psum_scatter(jnp.dot(factor_rows, weights, preferred_element_type=jnp...  144 us
    all_to_all x1, blocking collectives, on_device(): lax.all_to_all(picked, 'pair', split_axis=0, concat_axis=0, tiled=True)  104 us
    all_to_all x1, waiting for transfers between devices, on_device(): lax.all_to_all(send_blocks, 'pair', split_axis=0, concat_axis=0, tiled=True)  95.3 us
    all_gather x1, waiting for transfers between devices, on_device(): shard_rows = lax.all_gather(inter_share, 'pair', axis=0, tiled=True)  83.6 us
    unnamed x4, local copies, waits for them, and re-layouts  21.7 us
  transfers between devices with their start and end apart: 6, of which 6 were waited for; matrix products, arithmetic and copies ran while one was open for 1% of the time, Pallas kernels for 0%

profile of v1, /device:TPU:1, one launch (start us, length us, event | category | flops | bytes accessed | tf_op | source)
XLA Modules:
  0.0 724.3 jit_solution(12598169757977810213)
XLA Ops:
  6.5 0.8 add_bitcast_fusion
  7.3 0.8 select_reduce_fusion.3
  8.2 0.1 fusion.18
  8.2 0.1 reduce_window_sum.11
  8.3 0.2 select_reduce_fusion.2
  8.5 0.1 select_reduce_fusion.1
  8.7 0.1 stack.10
  8.8 0.2 stack.9
  9.0 0.7 copy.26
  9.6 13.2 %all-to-all-start = ((bf16[64,2,2]{1,2,0:T(2,128)(2,1)}), bf16[64,2,2]{1,2,0:T(2,128)(2,1)S(1)}, u32[]{:S(2)}, u32[]{:S(2)}) async-start(bf16[64,2,2]{1,2,0:T(2,128)(2,1)} %copy.26), calls=%async_computation | async-start | bytes 65536 | tf_op jit(solution)/shard_map/all_to_all | solution.py:58
  22.8 2.8 fusion.10
  25.6 3.2 copy.39
  28.8 3.2 all-to-all-done
  32.0 7.3 %all-to-all-start.1 = ((bf16[64,2,128,128]{3,2,1,0:T(8,128)(2,1)}), bf16[64,2,128,128]{3,2,1,0:T(8,128)(2,1)}, u32[]{:S(2)}, u32[]{:S(2)}) async-start(bf16[64,2,128,128]{3,2,1,0:T(8,128)(2,1)} %bitcast.84), calls=%async_computation.1 | async-start | bytes 8388608 | tf_op jit(solution)/shard_map/all_to_all | solution.py:57
  39.3 0.2 reduce-scatter.4.cloned.1.call-start
  39.6 0.1 copy.27
  39.7 0.1 copy.28
  39.8 0.1 sub.11
  40.0 95.3 %all-to-all-done.1 = bf16[64,2,128,128]{3,2,1,0:T(8,128)(2,1)} async-done(((bf16[64,2,128,128]{3,2,1,0:T(8,128)(2,1)}), bf16[64,2,128,128]{3,2,1,0:T(8,128)(2,1)}, u32[]{:S(2)}, u32[]{:S(2)}) %all-to-all-start.1) | async-done | bytes 4194336 | tf_op jit(solution)/shard_map/all_to_all | solution.py:57
  135.2 7.7 %copy.70 = bf16[16,8,128,128]{3,1,2,0:T(8,128)(2,1)} copy(bf16[16,8,128,128]{3,2,1,0:T(8,128)(2,1)} %bitcast.39) | data formatting | bytes 8388608
  142.9 6.4 copy.29
  149.3 3.8 convert_bitcast_fusion
  153.1 3.3 copy.30
  156.3 10.6 %convolution_bitcast_fusion = f32[2048,1024]{0,1:T(8,128)} fusion(bf16[256,8,8,128]{3,2,1,0:T(8,128)(2,1)} %bitcast.92, bf16[128,8,8,128]{3,2,1,0:T(8,128)(2,1)} %bitcast.90), kind=kOutput, calls=%fused_computation.3 | convolution fusion | flops 4294967296 | bytes 14680064 | tf_op jit(solution)/shard_map/dot_general | solution.py:78
  166.9 9.3 %copy.36 = f32[2048,1024]{1,0:T(8,128)} copy(f32[2048,1024]{0,1:T(8,128)} %convolution_bitcast_fusion) | data formatting | bytes 16777216
  176.2 0.0 reduce-scatter.4.cloned.1.call-update
  176.2 0.3 all-gather.2.cloned.1.call-start
  176.5 143.6 %reduce-scatter.4.cloned.1.call-done = f32[32,1024]{1,0:T(8,128)} async-done(((f32[2048,1024]{1,0:T(8,128)}), f32[32,1024]{1,0:T(8,128)}) %reduce-scatter.4.cloned.1.call-update) | async-done | bytes 131088 | tf_op jit(solution)/shard_map/reduce_scatter | solution.py:77
  320.2 1.5 convert_element_type.57
  321.7 0.0 all-gather.2.cloned.1.call-update
  321.7 83.6 %all-gather.2.cloned.1.call-done = bf16[2048,1024]{1,0:T(8,128)(2,1)} async-done(((bf16[32,1024]{1,0:T(8,128)(2,1)}), bf16[2048,1024]{1,0:T(8,128)(2,1)}) %all-gather.2.cloned.1.call-update) | async-done | bytes 4194320 | tf_op jit(solution)/shard_map/all_gather | solution.py:84
  405.4 6.5 copy.32
  411.9 7.5 %fusion.7 = f32[8,8,128,128]{3,2,1,0:T(8,128)S(1)} fusion(bf16[2048,8,128,1]{0,2,3,1:T(8,128)(2,1)} %bitcast.89, bf16[2048,8,128]{2,1,0:T(8,128)(2,1)} %bitcast.93), kind=kOutput, calls=%fused_computation.12 | convolution fusion | flops 4294967296 | bytes 12582912 | tf_op jit(solution)/shard_map/qAa,qCc->ACac/dot_general | solution.py:89
  419.4 1.3 collective-permute-start
  420.7 90.7 %collective-permute-done = f32[8,8,128,128]{3,2,1,0:T(8,128)S(1)} collective-permute-done((f32[8,8,128,128]{3,2,1,0:T(8,128)S(1)}, f32[8,8,128,128]{3,2,1,0:T(8,128)S(1)}, u32[]{:S(2)}, u32[]{:S(2)}) %collective-permute-start) | collective-permute-done | bytes 4194336 | tf_op jit(solution)/shard_map/ppermute | solution.py:16
  511.4 1.1 add.28
  512.5 2.8 collective-permute-start.1
  515.3 89.8 %collective-permute-done.1 = f32[8,8,128,128]{3,2,1,0:T(8,128)S(1)} collective-permute-done((f32[8,8,128,128]{3,2,1,0:T(8,128)S(1)}, f32[8,8,128,128]{3,2,1,0:T(8,128)S(1)}, u32[]{:S(2)}, u32[]{:S(2)}) %collective-permute-start.1) | collective-permute-done | bytes 4194336 | tf_op jit(solution)/shard_map/ppermute | solution.py:16
  605.1 0.9 add.29
  606.0 3.1 gather_fusion
  609.0 104.2 %all_to_all.15 = bf16[64,2,128,128]{3,2,1,0:T(8,128)(2,1)S(1)} all-to-all(bf16[64,2,128,128]{3,2,1,0:T(8,128)(2,1)} %bitcast.86), channel_id=1, replica_groups=mesh['pair'=64,'aux'=4] {'pair'}, dimensions={0} | all-to-all | bytes 8388608 | tf_op jit(solution)/shard_map/all_to_all | solution.py:95
  713.2 2.7 fusion.15
  716.0 1.6 copy.44
  (7 shorter events, 0.1 us)
Async XLA Ops:
  9.6 22.4 %all-to-all-start = ((bf16[64,2,2]{1,2,0:T(2,128)(2,1)}), bf16[64,2,2]{1,2,0:T(2,128)(2,1)S(1)}, u32[]{:S(2)}, u32[]{:S(2)}) async-start(bf16[64,2,2]{1,2,0:T(2,128)(2,1)} %copy.26), calls=%async_computation | async-start | bytes 65536 | tf_op jit(solution)/shard_map/all_to_all | solution.py:58
  32.0 103.2 %all-to-all-start.1 = ((bf16[64,2,128,128]{3,2,1,0:T(8,128)(2,1)}), bf16[64,2,128,128]{3,2,1,0:T(8,128)(2,1)}, u32[]{:S(2)}, u32[]{:S(2)}) async-start(bf16[64,2,128,128]{3,2,1,0:T(8,128)(2,1)} %bitcast.84), calls=%async_computation.1 | async-start | bytes 8388608 | tf_op jit(solution)/shard_map/all_to_all | solution.py:57
  39.3 280.8 %reduce-scatter.4.cloned.1.call-start = ((), (), s32[]{:S(2)}) async-start(), calls=%async_computation.5 | async-start | bytes 8519680 | tf_op jit(solution)/shard_map/reduce_scatter | solution.py:77
  176.2 229.1 %all-gather.2.cloned.1.call-start = ((), (), s32[]{:S(2)}) async-start(), calls=%async_computation.4 | async-start | bytes 4259840 | tf_op jit(solution)/shard_map/all_gather | solution.py:84
  419.4 92.0 %collective-permute-start = (f32[8,8,128,128]{3,2,1,0:T(8,128)S(1)}, f32[8,8,128,128]{3,2,1,0:T(8,128)S(1)}, u32[]{:S(2)}, u32[]{:S(2)}) collective-permute-start(f32[8,8,128,128]{3,2,1,0:T(8,128)S(1)} %fusion.7), channel_id=1, source_target_pairs={{0,1},{1,0},{2,3},{3,2},{4,5},{5,4},{6,7},{7,6},{8,9},{9,8},{10,11... | collective-permute-start | bytes 12582920 | tf_op jit(solution)/shard_map/ppermute | solution.py:16
  512.5 92.6 %collective-permute-start.1 = (f32[8,8,128,128]{3,2,1,0:T(8,128)S(1)}, f32[8,8,128,128]{3,2,1,0:T(8,128)S(1)}, u32[]{:S(2)}, u32[]{:S(2)}) collective-permute-start(f32[8,8,128,128]{3,2,1,0:T(8,128)S(1)} %add.28), channel_id=1, source_target_pairs={{0,2},{1,3},{2,0},{3,1},{4,6},{5,7},{6,4},{7,5},{8,10},{9,11},{10,... | collective-permute-start | bytes 12582920 | tf_op jit(solution)/shard_map/ppermute | solution.py:16
Sparse Core Ops, SparseCore 0:
  176.4 143.7 reduce-scatter.3
  323.3 82.0 all-gather.1
